TPU v7x, 256 devices: a whole 4x4x8 slice. The times are simulated.
256 devices in a mesh: tile: 4 (over y), proj: 16 (over x, z_hi, core), cuts: 4 (over z_lo).
Axes of the slice: x: 4, y: 4, z: 8 (z_hi: 2, z_lo: 4; z = z_hi * 4 + z_lo), core: 2. Of those that a mesh axis runs over, the one named last changes fastest.
Arguments:
- object_field: float32 [64, 2, 384, 2048], P(('proj', 'cuts'), None, None, 'tile'), may hold values from -5 to 5
- probe_field: float32 [2, 256, 256], replicated, may hold values from -6 to 6
- amplitudes: bfloat16 [64, 4, 6, 256, 256], P(('proj', 'cuts'), 'tile'), may hold values from 0 to 16
- pos_rows: int32 [64, 4, 6], P(('proj', 'cuts'), 'tile'), may hold values from 0 to 128
- pos_cols: int32 [64, 4, 6], P(('proj', 'cuts'), 'tile'), may hold values from 0 to 512
- counts: int32 [64, 4], P(('proj', 'cuts'), 'tile'), may hold values from 1 to 6, as said below
- admm_dual: float32 [64, 32, 2048], P(('proj', 'cuts'), None, 'tile'), may hold values from -4 to 4
- volume: float32 [32, 2048, 2048], P('cuts', ('tile', 'proj')), may hold values from -6 to 6
- proj_weights: bfloat16 [16, 2048, 2048], P(None, ('tile', 'proj')), may hold values from -0.125 to 0.125
- ray_weights: float32 [16, 2048], replicated, may hold values from -0.125 to 0.125
- angle_ids: int32 [64], replicated, may hold values from 0 to 15
Outputs:
- new_object: float32 [64, 2, 384, 2048], P(('proj', 'cuts'), None, None, 'tile')
- new_probe: float32 [2, 256, 256], replicated
- new_volume: float32 [32, 2048, 2048], P('cuts', ('tile', 'proj'))
Inputs may be any that keep to these rules, and one draw needn't show every extreme that they name: `counts`: every tile holds at least one live position and at most 6; exactly one tile of one projection holds 6, every other holds at most 3.
All inputs are finite; a program needn't handle non-finite values.
Results may differ from a plain program's by a relative error of at most 0.00095.
The roundings to bfloat16 on the way count: a program that leaves them out, or rounds other values in their place, can miss the bound.
Values may be sent and summed in bfloat16 or wider, within the bound.
A program may use at most 64 MiB of HBM per device.

v0:
```python
import math
import jax
import jax.numpy as jnp
from jax import lax
from jax.sharding import PartitionSpec as P

PB = 256
tomo_step = 1.0


def shifted(value, axis, steps):
    count = lax.axis_size(axis)
    leading, last = (max(0, -steps), min(count, count - steps))
    return lax.ppermute(value, axis, [(source, source + steps) for source in range(leading, last)])


def dft_tables(side):
    indices = jnp.arange(side, dtype=jnp.int32)
    products = indices[:, None] * indices[None, :] % side
    phase_angle = products.astype(jnp.float32) * (2.0 * math.pi / side)
    norm_factor = 1.0 / math.sqrt(side)
    return (
        (jnp.cos(phase_angle) * norm_factor).astype(jnp.bfloat16),
        (-jnp.sin(phase_angle) * norm_factor).astype(jnp.bfloat16),
    )


def matmul(left, right):
    return jnp.dot(left, right, preferred_element_type=jnp.float32)


def complex_matmul(left_real, left_imag, right_real, right_imag):
    out_real = matmul(left_real, right_real) - matmul(left_imag, right_imag)
    out_imag = matmul(left_real, right_imag) + matmul(left_imag, right_real)
    return (out_real, out_imag)


def patch_terms(patch_real, patch_imag, probe_real, probe_imag, amplitude, dft_real, dft_imag):
    wave_real = (probe_real * patch_real - probe_imag * patch_imag).astype(jnp.bfloat16)
    wave_imag = (probe_real * patch_imag + probe_imag * patch_real).astype(jnp.bfloat16)
    half_real, half_imag = complex_matmul(dft_real, dft_imag, wave_real, wave_imag)
    half_real = half_real.astype(jnp.bfloat16)
    half_imag = half_imag.astype(jnp.bfloat16)
    far_real, far_imag = complex_matmul(half_real, half_imag, dft_real, dft_imag)
    modulus = jnp.sqrt(far_real * far_real + far_imag * far_imag + 0.25)
    factor = amplitude.astype(jnp.float32) / modulus - 1.0
    diff_real = (far_real * factor).astype(jnp.bfloat16)
    diff_imag = (far_imag * factor).astype(jnp.bfloat16)
    conj_imag = -dft_imag
    back_half_real, back_half_imag = complex_matmul(dft_real, conj_imag, diff_real, diff_imag)
    back_half_real = back_half_real.astype(jnp.bfloat16)
    back_half_imag = back_half_imag.astype(jnp.bfloat16)
    back_real, back_imag = complex_matmul(back_half_real, back_half_imag, dft_real, conj_imag)
    object_real = probe_real * back_real + probe_imag * back_imag
    object_imag = probe_real * back_imag - probe_imag * back_real
    probe_grad_real = patch_real * back_real + patch_imag * back_imag
    probe_grad_imag = patch_real * back_imag - patch_imag * back_real
    energy = jnp.mean(patch_real * patch_real + patch_imag * patch_imag)
    return (
        jnp.stack([object_real, object_imag]),
        jnp.stack([probe_grad_real, probe_grad_imag]),
        energy,
    )


def tile_edges(values, offset):
    return shifted(values, "tile", offset)


def on_device(
    object_field,
    probe_field,
    amplitudes,
    pos_rows,
    pos_cols,
    counts,
    admm_dual,
    volume,
    proj_weights,
    ray_weights,
    angle_ids,
):
    half_side = PB // 2
    own_object = object_field[0]
    tile_cols = own_object.shape[2]
    from_left = tile_edges(own_object[:, :, tile_cols - half_side :], 1)
    from_right = tile_edges(own_object[:, :, :half_side], -1)
    extended = jnp.concatenate([from_left, own_object, from_right], axis=2)
    dft_real, dft_imag = dft_tables(PB)
    probe_real = probe_field[0]
    probe_imag = probe_field[1]
    zero_index = jnp.zeros((), jnp.int32)
    live_count = counts[0, 0]
    slot_total = amplitudes.shape[2]

    def slot_step(slot_index, state_tuple, weight):
        grad_sum, probe_sum, energy_sum = state_tuple
        anchor = (zero_index, pos_rows[0, 0, slot_index], pos_cols[0, 0, slot_index])
        object_patch = lax.dynamic_slice(extended, anchor, (2, PB, PB))
        object_part, probe_part, energy = patch_terms(
            object_patch[0],
            object_patch[1],
            probe_real,
            probe_imag,
            amplitudes[0, 0, slot_index],
            dft_real,
            dft_imag,
        )
        current = lax.dynamic_slice(grad_sum, anchor, (2, PB, PB))
        grad_sum = lax.dynamic_update_slice(grad_sum, current + weight * object_part, anchor)
        return (grad_sum, probe_sum + weight * probe_part, energy_sum + weight * energy)

    running = (
        jnp.zeros(extended.shape, jnp.float32),
        jnp.zeros((2, PB, PB), jnp.float32),
        jnp.zeros((), jnp.float32),
    )
    running = lax.fori_loop(
        0,
        slot_total,
        lambda slot_index, state_tuple: slot_step(
            slot_index, state_tuple, (slot_index < live_count).astype(jnp.float32)
        ),
        running,
    )
    grad_sum, probe_sum, energy_sum = running
    to_right_edge = tile_edges(grad_sum[:, :, :half_side], -1)
    to_left_edge = tile_edges(grad_sum[:, :, tile_cols + half_side :], 1)
    own_cells = grad_sum[:, :, half_side : half_side + tile_cols]
    own_cells = own_cells.at[:, :, :half_side].add(to_left_edge)
    own_cells = own_cells.at[:, :, tile_cols - half_side :].add(to_right_edge)
    probe_grad, energy = lax.psum((probe_sum, energy_sum), ("tile", "proj", "cuts"))
    new_probe = probe_field + probe_grad / (energy + 1e-05)
    probe_peak = jnp.max(probe_real * probe_real + probe_imag * probe_imag)
    new_object = (own_object + own_cells / (probe_peak + 1e-05))[None]
    slab_total = admm_dual.shape[1]
    first_row = (own_object.shape[1] - slab_total) // 2
    slab_values = new_object[:, 1, first_row : first_row + slab_total, :] + admm_dual
    arrived = lax.all_to_all(
        lax.all_to_all(slab_values, "proj", split_axis=2, concat_axis=0, tiled=True),
        "cuts",
        split_axis=1,
        concat_axis=0,
        tiled=True,
    )
    proj_count = lax.axis_size("proj")
    cuts_count = lax.axis_size("cuts")
    slab_dev = arrived.shape[1]
    u_share = arrived.shape[2]
    projections = proj_count * cuts_count
    arrived = arrived.reshape(cuts_count, proj_count, slab_dev, u_share).transpose(1, 0, 2, 3)
    target = (
        arrived.reshape(projections, slab_dev, u_share)
        .transpose(2, 0, 1)
        .reshape(u_share, projections * slab_dev)
    )
    angle_count = ray_weights.shape[0]
    x_share = volume.shape[1]
    width = volume.shape[2]
    onehot = (angle_ids[:, None] == jnp.arange(angle_count, dtype=jnp.int32)[None, :]).astype(
        jnp.float32
    )
    ray_table = jnp.dot(
        onehot, ray_weights, precision=lax.Precision.HIGHEST, preferred_element_type=jnp.float32
    )
    ray_sums = jnp.einsum("zxy,ay->azx", volume, ray_table, precision=lax.Precision.HIGHEST).astype(
        jnp.bfloat16
    )
    spread = onehot.astype(jnp.bfloat16)[:, :, None, None] * ray_sums[:, None, :, :]
    spread = spread.transpose(1, 3, 0, 2).reshape(angle_count * x_share, projections * slab_dev)
    weight_flat = proj_weights.reshape(angle_count * x_share, width)
    partial_term = lax.dot_general(
        weight_flat, spread, (((0,), (0,)), ((), ())), preferred_element_type=jnp.float32
    )
    row_start = lax.axis_index(("tile", "proj")) * u_share
    own_rows = lax.dynamic_slice_in_dim(partial_term, row_start, u_share, 0)
    partial_term = lax.dynamic_update_slice_in_dim(partial_term, own_rows - target, row_start, 0)
    summed = lax.psum(partial_term, ("tile", "proj"))
    residue = summed.astype(jnp.bfloat16)
    backproj = matmul(weight_flat, residue)
    backproj = backproj.reshape(angle_count, x_share, projections, slab_dev)
    back_sums = jnp.einsum("gxaz,ag->azx", backproj, onehot, precision=lax.Precision.HIGHEST)
    gradient = jnp.einsum("azx,ay->zxy", back_sums, ray_table, precision=lax.Precision.HIGHEST)
    new_volume = volume - tomo_step * gradient
    return (new_object, new_probe, new_volume)


def solution(mesh):
    in_specs = (
        P(("proj", "cuts"), None, None, "tile"),
        P(),
        P(("proj", "cuts"), "tile", None, None, None),
        P(("proj", "cuts"), "tile", None),
        P(("proj", "cuts"), "tile", None),
        P(("proj", "cuts"), "tile"),
        P(("proj", "cuts"), None, "tile"),
        P("cuts", ("tile", "proj"), None),
        P(None, ("tile", "proj"), None),
        P(),
        P(),
    )
    out_specs = (P(("proj", "cuts"), None, None, "tile"), P(), P("cuts", ("tile", "proj"), None))
    return jax.shard_map(
        on_device, mesh=mesh, in_specs=in_specs, out_specs=out_specs, check_vma=False
    )
```

profile of v0, /device:TPU:64, one launch (start us, length us, event | category | flops | bytes accessed | tf_op | source)
XLA Modules:
  0.0 1082.3 jit_solution(16087223290670484655)
XLA Ops:
  7.2 3.2 copy.38
  10.4 2.1 fusion.135
  13.8 5.3 collective-permute-start
  20.4 3.4 fusion.127
  25.5 4.1 mul.437
  30.3 3.0 pad_maximum_fusion
  34.9 254.5 %while.23 = (s32[]{:T(128)}, f32[2,384,768]{1,2,0:T(8,128)}, f32[2,256,256]{2,1,0:T(8,128)}, f32[]{:T(128)}, s32[1,1,6]{2,1,0:T(1,128)S(1)}, /*index=5*/s32[1,1,...) while((s32[]{:T(128)}, f32[2,384,768]{1,2,0:T(8,128)}, ...), condition=%wide.region_2.3_spmd.clone.clone, body=%wide.region_0.2_spmd.clone.clone.sunk | while | flops 558956544 | bytes 22151564 | solution.py:118
  40.9 2.0 constant_dynamic-slice_fusion.9
  53.8 2.1 multiply_convert_fusion.39
  64.0 2.2 fusion.233
  68.2 6.5 dynamic_update_slice.17
  83.2 2.0 constant_dynamic-slice_fusion.9
  96.1 2.1 multiply_convert_fusion.39
  106.3 2.2 fusion.233
  110.5 6.5 dynamic_update_slice.17
  117.0 2.1 fusion.235
  125.7 2.0 constant_dynamic-slice_fusion.9
  138.6 2.1 multiply_convert_fusion.39
  148.8 2.2 fusion.233
  153.0 6.1 dynamic_update_slice.17
  159.1 2.1 fusion.235
  167.7 2.0 constant_dynamic-slice_fusion.9
  180.6 2.1 multiply_convert_fusion.39
  190.8 2.2 fusion.233
  195.0 6.6 dynamic_update_slice.17
  201.6 2.1 fusion.235
  210.2 2.0 constant_dynamic-slice_fusion.9
  223.2 2.1 multiply_convert_fusion.39
  233.3 2.2 fusion.233
  237.5 6.5 dynamic_update_slice.17
  244.1 2.1 fusion.235
  265.6 2.1 multiply_convert_fusion.39
  275.8 2.2 fusion.233
  280.0 6.5 dynamic_update_slice.17
  286.6 2.1 fusion.235
  291.5 2.8 collective-permute-start.2
  295.6 4.3 fusion.138
  301.4 2.7 slice.97
  313.8 9.8 all-to-all-start
  323.7 79.2 %psum.22 = f32[]{:T(128)} all-reduce(f32[]{:T(128)} %get-tuple-element.384), channel_id=1, replica_groups=mesh['tile'=4,'proj'=16,'cuts'=4] {'tile','proj','cuts'}, use_global_device_ids=true, to_apply=%region_5.6 | all-reduce | flops 1 | bytes 8 | tf_op jit(solution)/shard_map/psum | solution.py:132
  405.8 6.0 all-to-all-start.1
  411.8 145.5 %all-reduce.3.cloned.1.call-done = f32[2,256,256]{2,1,0:T(8,128)} async-done(((f32[2,256,256]{2,1,0:T(8,128)}), f32[2,256,256]{2,1,0:T(8,128)}) %all-reduce.3.cloned.1.call-update) | async-done | bytes 524304 | tf_op jit(solution)/shard_map/psum | solution.py:132
  559.2 3.0 copy.48
  566.2 495.1 %all-reduce.4 = bf16[2048,512]{0,1:T(8,128)(2,1)} all-reduce(f32[2048,512]{0,1:T(8,128)} %dynamic_update_slice.13), channel_id=1, replica_groups=mesh['tile'=4,'proj'=16,'cuts'=4] {'tile','proj'}, use_global_device_ids=true, to_apply=%region_6.7 | all-reduce | flops 1048576 | bytes 6291456 | tf_op jit(solution)/shard_map/psum | solution.py:178
  1061.4 2.9 fusion.124
  1064.2 2.5 reshape.122
  1066.7 3.8 fusion.130
  1070.7 4.7 convolution_subtract_fusion.4
  (211 shorter events, 166.3 us)
Async XLA Ops:
  7.2 288.4 %copy-start = (bf16[16,32,2048]{2,1,0:T(8,128)(2,1)S(1)}, bf16[16,32,2048]{2,1,0:T(8,128)(2,1)}, u32[]{:S(2)}) copy-start(bf16[16,32,2048]{2,1,0:T(8,128)(2,1)} %param.25) | copy-start | bytes 6291460
  7.2 11.9 %copy-start.12 = (s32[64]{0:T(128)S(1)}, s32[64]{0:T(128)}, u32[]{:S(2)}) copy-start(s32[64]{0:T(128)} %param.27) | copy-start | bytes 772
  7.2 11.9 %copy-start.8 = (f32[16,2048]{1,0:T(8,128)S(1)}, f32[16,2048]{1,0:T(8,128)}, u32[]{:S(2)}) copy-start(f32[16,2048]{1,0:T(8,128)} %param.26) | copy-start | bytes 393220
  7.2 550.1 %all-reduce.3.cloned.1.call-start = ((), (), s32[]{:S(2)}) async-start(), calls=%async_computation.2 | async-start | bytes 1048576 | tf_op jit(solution)/shard_map/psum | solution.py:132
  12.5 17.9 %collective-permute-start.1 = (f32[2,384,128]{1,2,0:T(8,128)}, f32[2,384,128]{1,2,0:T(8,128)S(1)}, u32[]{:S(2)}, u32[]{:S(2)}) collective-permute-start(f32[2,384,128]{1,2,0:T(8,128)} %get-tuple-element.557), channel_id=1, source_target_pairs={{64,0},{128,64},{192,128},{65,1},{129,65},{193,129},{66,2},{130,66... | collective-permute-start | bytes 1179656 | tf_op jit(solution)/shard_map/ppermute | solution.py:14
  13.8 16.6 %collective-permute-start = (f32[2,384,128]{1,2,0:T(8,128)}, f32[2,384,128]{1,2,0:T(8,128)}, u32[]{:S(2)}, u32[]{:S(2)}) collective-permute-start(f32[2,384,128]{1,2,0:T(8,128)} %get-tuple-element.556), channel_id=1, source_target_pairs={{0,64},{64,128},{128,192},{1,65},{65,129},{129,193},{2,66},{66,130... | collective-permute-start | bytes 1179656 | tf_op jit(solution)/shard_map/ppermute | solution.py:14
  19.6 0.8 copy-start.6
  23.9 5.7 copy-start.4
  33.4 1.6 copy-start.10
  33.4 1.6 copy-start.11
  60.5 3.5 copy-start.1
  102.8 3.4 copy-start.1
  145.3 3.5 copy-start.1
  187.4 3.5 copy-start.1
  229.9 3.4 copy-start.1
  272.4 3.4 copy-start.1
  291.5 12.6 %collective-permute-start.2 = (f32[2,384,128]{1,2,0:T(8,128)}, f32[2,384,128]{1,2,0:T(8,128)}, u32[]{:S(2)}, u32[]{:S(2)}) collective-permute-start(f32[2,384,128]{1,2,0:T(8,128)} %get-tuple-element.555), channel_id=1, source_target_pairs={{0,64},{64,128},{128,192},{1,65},{65,129},{129,193},{2,66},{66,130... | collective-permute-start | bytes 1179656 | tf_op jit(solution)/shard_map/ppermute | solution.py:14
  294.3 11.9 %collective-permute-start.3 = (f32[2,384,128]{1,2,0:T(8,128)S(1)}, f32[2,384,128]{1,2,0:T(8,128)}, u32[]{:S(2)}, u32[]{:S(2)}) collective-permute-start(f32[2,384,128]{1,2,0:T(8,128)S(1)} %get-tuple-element.554), channel_id=1, source_target_pairs={{64,0},{128,64},{192,128},{65,1},{129,65},{193,129},{66,2},{130,66... | collective-permute-start | bytes 1179656 | tf_op jit(solution)/shard_map/ppermute | solution.py:14
  295.6 4.3 copy-start.9
  295.6 4.5 copy-start.5
  304.0 4.0 copy-start.2
  309.7 1.1 copy-start.3
  313.8 89.7 %all-to-all-start = ((f32[16,1,1024]{2,1,0:T(1,128)}), f32[16,1,1024]{2,1,0:T(1,128)S(1)}, u32[]{:S(2)}, u32[]{:S(2)}) async-start(f32[16,1,1024]{2,1,0:T(1,128)} %reshape.128), calls=%async_computation | async-start | bytes 131072 | tf_op jit(solution)/shard_map/all_to_all | solution.py:140
  405.8 156.4 %all-to-all-start.1 = ((f32[4,1,4096]{2,1,0:T(1,128)}), f32[4,1,4096]{2,1,0:T(1,128)S(1)}, u32[]{:S(2)}, u32[]{:S(2)}) async-start(f32[4,1,4096]{2,1,0:T(1,128)} %reshape.130), calls=%async_computation.1 | async-start | bytes 131072 | tf_op jit(solution)/shard_map/all_to_all | solution.py:139
  1066.7 4.0 copy-start.7
Sparse Core Ops, SparseCore 0:
  304.2 253.0 all-reduce.2
where the time goes:
time: 1090 us; the launch traced here: 1080 us
  blocking collectives  574 us (53%)
  waiting for transfers between devices  146 us (13%)
  matrix products  141 us (13%)
  local copies, waits for them, and re-layouts  101 us (9%)
  other arithmetic  45.9 us (4%)
  loops' own time  31.6 us (3%)
  starting transfers between devices  26.6 us (2%)
  between operations  15.6 us (1%)
    psum x1, blocking collectives, on_device(): summed = lax.psum(partial_term, ('tile', 'proj'))  495 us
    psum x1, waiting for transfers between devices, on_device(): lax.psum((probe_sum, energy_sum), ('tile', 'proj', 'cuts'))  145 us
    dot_general x97, matrix products, matmul(): return jnp.dot(left, right, preferred_element_type=jnp.float32)  125 us
    psum x1, blocking collectives, on_device(): lax.psum((probe_sum, energy_sum), ('tile', 'proj', 'cuts'))  79.2 us
    dynamic_update_slice x12, local copies, waits for them, and re-layouts, slot_step(): lax.dynamic_update_slice(grad_sum, current + weight * object_part, anchor)  39.9 us
    another operation x1, loops' own time, on_device(): lax.fori_loop(0, slot_total, lambda slot_index, state_tuple: slot_step(sl...  31.6 us
  transfers between devices with their start and end apart: 7, of which 2 were waited for; matrix products, arithmetic and copies ran while one was open for 3% of the time, Pallas kernels for 0%

commit v1 on v0

--- a/solution.py
+++ b/solution.py
@@ -175,7 +175,7 @@
     row_start = lax.axis_index(("tile", "proj")) * u_share
     own_rows = lax.dynamic_slice_in_dim(partial_term, row_start, u_share, 0)
     partial_term = lax.dynamic_update_slice_in_dim(partial_term, own_rows - target, row_start, 0)
-    summed = lax.psum(partial_term, ("tile", "proj"))
+    summed = lax.psum(lax.psum(partial_term, "tile"), "proj")
     residue = summed.astype(jnp.bfloat16)
     backproj = matmul(weight_flat, residue)
     backproj = backproj.reshape(angle_count, x_share, projections, slab_dev)

time: 1090 us -> 903 us (0.83)
  the two profiles are of different devices: /device:TPU:64 before, /device:TPU:8 now
where the time goes in v1:
time: 903 us; the launch traced here: 899 us
  waiting for transfers between devices  273 us (30%)
  blocking collectives  270 us (30%)
  matrix products  141 us (16%)
  local copies, waits for them, and re-layouts  101 us (11%)
  other arithmetic  41 us (5%)
  loops' own time  30.5 us (3%)
  starting transfers between devices  27.2 us (3%)
  between operations  15.6 us (2%)
    psum x1, blocking collectives, on_device(): summed = lax.psum(lax.psum(partial_term, 'tile'), 'proj')  197 us
    psum x1, waiting for transfers between devices, on_device(): lax.psum((probe_sum, energy_sum), ('tile', 'proj', 'cuts'))  159 us
    dot_general x97, matrix products, matmul(): return jnp.dot(left, right, preferred_element_type=jnp.float32)  125 us
    psum x1, waiting for transfers between devices, on_device(): summed = lax.psum(lax.psum(partial_term, 'tile'), 'proj')  93.1 us
    psum x1, blocking collectives, on_device(): lax.psum((probe_sum, energy_sum), ('tile', 'proj', 'cuts'))  73.3 us
    dynamic_update_slice x12, local copies, waits for them, and re-layouts, slot_step(): lax.dynamic_update_slice(grad_sum, current + weight * object_part, anchor)  39.8 us
    another operation x1, loops' own time, on_device(): lax.fori_loop(0, slot_total, lambda slot_index, state_tuple: slot_step(sl...  30.5 us
  transfers between devices with their start and end apart: 8, of which 7 were waited for; matrix products, arithmetic and copies ran while one was open for 3% of the time, Pallas kernels for 0%

profile of v1, /device:TPU:8, one launch (start us, length us, event | category | flops | bytes accessed | tf_op | source)
XLA Modules:
  0.0 899.1 jit_solution(7253220733620778856)
XLA Ops:
  7.2 3.2 copy.38
  12.4 4.1 collective-permute-start.1
  20.4 4.9 collective-permute-done.1
  27.4 2.6 pad_maximum_fusion
  31.5 252.9 %while.23 = (s32[]{:T(128)}, f32[2,384,768]{1,2,0:T(8,128)}, f32[2,256,256]{2,1,0:T(8,128)}, f32[]{:T(128)}, s32[1,1,6]{2,1,0:T(1,128)S(1)}, /*index=5*/s32[1,1,...) while((s32[]{:T(128)}, f32[2,384,768]{1,2,0:T(8,128)}, ...), condition=%wide.region_2.3_spmd.clone.clone, body=%wide.region_0.2_spmd.clone.clone.sunk | while | flops 558956544 | bytes 22151564 | solution.py:118
  50.2 2.1 multiply_convert_fusion.39
  60.4 2.2 fusion.233
  64.6 6.5 dynamic_update_slice.17
  92.3 2.1 multiply_convert_fusion.39
  102.5 2.2 fusion.233
  106.7 6.5 dynamic_update_slice.17
  113.2 2.1 fusion.235
  134.5 2.1 multiply_convert_fusion.39
  144.7 2.2 fusion.233
  148.9 6.1 dynamic_update_slice.17
  155.0 2.1 fusion.235
  176.4 2.1 multiply_convert_fusion.39
  186.5 2.2 fusion.233
  190.7 6.5 dynamic_update_slice.17
  197.2 2.1 fusion.235
  218.5 2.1 multiply_convert_fusion.39
  228.7 2.2 fusion.233
  232.9 6.5 dynamic_update_slice.17
  239.4 2.1 fusion.235
  260.8 2.1 multiply_convert_fusion.39
  270.9 2.2 fusion.233
  275.1 6.5 dynamic_update_slice.17
  281.7 2.1 fusion.235
  284.5 2.1 fusion.134
  286.6 2.9 collective-permute-start.2
  289.5 3.5 fusion.127
  294.6 3.7 collective-permute-start.3
  301.2 5.6 collective-permute-done.3
  311.3 11.3 %all-to-all-start = ((f32[16,1,1024]{2,1,0:T(1,128)}), f32[16,1,1024]{2,1,0:T(1,128)S(1)}, u32[]{:S(2)}, u32[]{:S(2)}) async-start(f32[16,1,1024]{2,1,0:T(1,128)} %reshape.128), calls=%async_computation | async-start | bytes 131072 | tf_op jit(solution)/shard_map/all_to_all | solution.py:140
  324.2 3.4 mul.437
  327.6 5.0 all-to-all-done
  336.5 3.3 all-to-all-start.1
  339.8 3.2 fusion.138
  343.1 2.4 all-to-all-done.1
  349.6 73.3 %psum.29 = f32[]{:T(128)} all-reduce(f32[]{:T(128)} %get-tuple-element.384), channel_id=1, replica_groups=mesh['tile'=4,'proj'=16,'cuts'=4] {'tile','proj','cuts'}, use_global_device_ids=true, to_apply=%region_5.6 | all-reduce | flops 1 | bytes 8 | tf_op jit(solution)/shard_map/psum | solution.py:132
  423.5 159.5 %all-reduce.4.cloned.1.call-done = f32[2,256,256]{2,1,0:T(8,128)} async-done(((f32[2,256,256]{2,1,0:T(8,128)}), f32[2,256,256]{2,1,0:T(8,128)}) %all-reduce.4.cloned.1.call-update) | async-done | bytes 524304 | tf_op jit(solution)/shard_map/psum | solution.py:132
  584.9 3.0 copy.48
  587.9 93.1 %all-reduce.6.cloned.1.call-done = f32[2048,512]{0,1:T(8,128)} async-done(((f32[2048,512]{0,1:T(8,128)}), f32[2048,512]{0,1:T(8,128)}) %all-reduce.6.cloned.1.call-update) | async-done | bytes 4194320 | tf_op jit(solution)/shard_map/psum | solution.py:178
  681.0 197.2 %all-reduce.7 = bf16[2048,512]{0,1:T(8,128)(2,1)} all-reduce(f32[2048,512]{0,1:T(8,128)} %all-reduce.6.cloned.1.call-done), channel_id=1, replica_groups=mesh['tile'=4,'proj'=16,'cuts'=4] {'proj'}, use_global_device_ids=true, to_apply=%region_7.8 | all-reduce | flops 1048576 | bytes 6291456 | tf_op jit(solution)/shard_map/psum | solution.py:178
  878.2 2.9 fusion.124
  881.1 2.5 reshape.122
  883.6 3.8 fusion.130
  887.6 4.7 convolution_subtract_fusion.4
  (214 shorter events, 176.8 us)
Async XLA Ops:
  7.2 332.6 %copy-start = (bf16[16,32,2048]{2,1,0:T(8,128)(2,1)S(1)}, bf16[16,32,2048]{2,1,0:T(8,128)(2,1)}, u32[]{:S(2)}) copy-start(bf16[16,32,2048]{2,1,0:T(8,128)(2,1)} %param.25) | copy-start | bytes 6291460
  7.2 11.3 %copy-start.8 = (f32[16,2048]{1,0:T(8,128)S(1)}, f32[16,2048]{1,0:T(8,128)}, u32[]{:S(2)}) copy-start(f32[16,2048]{1,0:T(8,128)} %param.26) | copy-start | bytes 393220
  7.2 11.3 %copy-start.12 = (s32[64]{0:T(128)S(1)}, s32[64]{0:T(128)}, u32[]{:S(2)}) copy-start(s32[64]{0:T(128)} %param.27) | copy-start | bytes 772
  7.2 12.5 %copy-start.5 = (f32[2,256,256]{2,1,0:T(8,128)S(1)}, f32[2,256,256]{2,1,0:T(8,128)}, u32[]{:S(2)}) copy-start(f32[2,256,256]{2,1,0:T(8,128)} %param.18) | copy-start | bytes 1572868
  12.4 12.9 %collective-permute-start.1 = (f32[2,384,128]{1,2,0:T(8,128)}, f32[2,384,128]{1,2,0:T(8,128)S(1)}, u32[]{:S(2)}, u32[]{:S(2)}) collective-permute-start(f32[2,384,128]{1,2,0:T(8,128)} %get-tuple-element.557), channel_id=1, source_target_pairs={{64,0},{128,64},{192,128},{65,1},{129,65},{193,129},{66,2},{130,66... | collective-permute-start | bytes 1179656 | tf_op jit(solution)/shard_map/ppermute | solution.py:14
  16.5 10.9 %collective-permute-start = (f32[2,384,128]{1,2,0:T(8,128)}, f32[2,384,128]{1,2,0:T(8,128)}, u32[]{:S(2)}, u32[]{:S(2)}) collective-permute-start(f32[2,384,128]{1,2,0:T(8,128)} %get-tuple-element.556), channel_id=1, source_target_pairs={{0,64},{64,128},{128,192},{1,65},{65,129},{129,193},{2,66},{66,130... | collective-permute-start | bytes 1179656 | tf_op jit(solution)/shard_map/ppermute | solution.py:14
  18.5 8.9 copy-start.2
  30.0 1.6 copy-start.10
  30.0 1.6 copy-start.11
  56.9 3.4 copy-start.1
  99.0 3.5 copy-start.1
  141.2 3.5 copy-start.1
  183.1 3.5 copy-start.1
  225.3 3.4 copy-start.1
  267.5 3.4 copy-start.1
  284.5 8.7 copy-start.9
  284.5 8.9 copy-start.6
  286.6 13.4 %collective-permute-start.2 = (f32[2,384,128]{1,2,0:T(8,128)}, f32[2,384,128]{1,2,0:T(8,128)}, u32[]{:S(2)}, u32[]{:S(2)}) collective-permute-start(f32[2,384,128]{1,2,0:T(8,128)} %get-tuple-element.555), channel_id=1, source_target_pairs={{0,64},{64,128},{128,192},{1,65},{65,129},{129,193},{2,66},{66,130... | collective-permute-start | bytes 1179656 | tf_op jit(solution)/shard_map/ppermute | solution.py:14
  294.6 12.2 %collective-permute-start.3 = (f32[2,384,128]{1,2,0:T(8,128)}, f32[2,384,128]{1,2,0:T(8,128)S(1)}, u32[]{:S(2)}, u32[]{:S(2)}) collective-permute-start(f32[2,384,128]{1,2,0:T(8,128)} %get-tuple-element.554), channel_id=1, source_target_pairs={{64,0},{128,64},{192,128},{65,1},{129,65},{193,129},{66,2},{130,66... | collective-permute-start | bytes 1179656 | tf_op jit(solution)/shard_map/ppermute | solution.py:14
  298.3 8.5 copy-start.3
  307.0 1.2 copy-start.4
  311.3 21.4 %all-to-all-start = ((f32[16,1,1024]{2,1,0:T(1,128)}), f32[16,1,1024]{2,1,0:T(1,128)S(1)}, u32[]{:S(2)}, u32[]{:S(2)}) async-start(f32[16,1,1024]{2,1,0:T(1,128)} %reshape.128), calls=%async_computation | async-start | bytes 131072 | tf_op jit(solution)/shard_map/all_to_all | solution.py:140
  322.6 260.5 %all-reduce.4.cloned.1.call-start = ((), (), s32[]{:S(2)}) async-start(), calls=%async_computation.2 | async-start | bytes 1048576 | tf_op jit(solution)/shard_map/psum | solution.py:132
  336.5 9.0 %all-to-all-start.1 = ((f32[4,1,4096]{2,1,0:T(1,128)}), f32[4,1,4096]{2,1,0:T(1,128)S(1)}, u32[]{:S(2)}, u32[]{:S(2)}) async-start(f32[4,1,4096]{2,1,0:T(1,128)} %reshape.130), calls=%async_computation.1 | async-start | bytes 131072 | tf_op jit(solution)/shard_map/all_to_all | solution.py:139
  339.8 341.3 %all-reduce.6.cloned.1.call-start = ((), (), s32[]{:S(2)}) async-start(), calls=%async_computation.3 | async-start | bytes 8388608 | tf_op jit(solution)/shard_map/psum | solution.py:178
  883.6 4.0 copy-start.7
Sparse Core Ops, SparseCore 0:
  329.4 253.5 all-reduce.3
  585.4 95.5 all-reduce.5
